TPU v7x, 32 devices: a whole 2x2x4 slice. The times are simulated.
32 devices in a mesh: dp: 8 (over y, x, core), fsdp: 4 (over z).
Axes of the slice: x: 2, y: 2, z: 4, core: 2. Of those that a mesh axis runs over, the one named last changes fastest.
Arguments:
- tokens: bfloat16 [16384, 1024], P(('dp', 'fsdp')), may hold values from -20 to 20
- w_qkv: bfloat16 [1024, 3072], P('fsdp'), may hold values from -0.1875 to 0.1875
- w_out: bfloat16 [1024, 1024], P('fsdp'), may hold values from -0.1875 to 0.1875
- doc_blocks: int32 [32, 4], P(('dp', 'fsdp')), may hold values from 0 to 1, never falling along the last dimension, each value on 1 to 3 neighbouring positions
- cotangent: bfloat16 [16384, 1024], P(('dp', 'fsdp')), may hold values from -6 to 6
Outputs:
- output: bfloat16 [16384, 1024], P(('dp', 'fsdp'))
- grad_tokens: bfloat16 [16384, 1024], P(('dp', 'fsdp'))
- grad_w_qkv: float32 [1024, 3072], P('fsdp')
- grad_w_out: float32 [1024, 1024], P('fsdp')
Inputs may be any that keep to these rules, and one draw needn't show every extreme that they name: `doc_blocks`: ids never fall along a sequence; each of the 2 documents of a sequence covers 1 to 3 blocks.
All inputs are finite; a program needn't handle non-finite values.
Results may differ from a plain program's by a relative error of at most 0.012.
Values may be sent and summed in bfloat16 or wider, within the bound.
A program may use at most 128 MiB of HBM per device.

v0:
```python
import math
import jax
import jax.numpy as jnp
from jax import lax
from jax.sharding import PartitionSpec as P

H = 8
NEG_FILL = -1e30
CONTRACT_ROWS = (((0,), (0,)), ((), ()))
CONTRACT_COLS = (((1,), (1,)), ((), ()))


def row_mask(doc_ids, row_count):
    block_len = row_count // doc_ids.shape[0]
    doc_rows = jnp.repeat(doc_ids, block_len, total_repeat_length=row_count)
    position = jnp.arange(row_count, dtype=jnp.int32)
    causal = position[None, :] <= position[:, None]
    return causal & (doc_rows[None, :] == doc_rows[:, None])


def split_heads(matrix, head_count):
    return matrix.reshape(matrix.shape[0], head_count, matrix.shape[1] // head_count)


def attend_forward(query_rows, key_rows, value_rows, allowed, head_count):
    row_count = query_rows.shape[0]
    query_heads = split_heads(query_rows, head_count)
    key_heads = split_heads(key_rows, head_count)
    value_heads = split_heads(value_rows, head_count)
    score_scale = query_heads.shape[2] ** (-0.5)
    scores = (
        jnp.einsum("qhd,khd->hqk", query_heads, key_heads, preferred_element_type=jnp.float32)
        * score_scale
    )
    scores = jnp.where(allowed[None], scores, NEG_FILL)
    highest = jnp.max(scores, axis=-1, keepdims=True)
    expvals = jnp.exp(scores - highest)
    attn_probs = expvals / jnp.sum(expvals, axis=-1, keepdims=True)
    probs_half = attn_probs.astype(jnp.bfloat16)
    mixed = jnp.einsum("hqk,khd->qhd", probs_half, value_heads, preferred_element_type=jnp.float32)
    return (mixed.astype(jnp.bfloat16).reshape(row_count, -1), attn_probs, probs_half)


def attend_backward(
    query_rows, key_rows, value_rows, attn_probs, probs_half, grad_mixed, head_count
):
    row_count = query_rows.shape[0]
    query_heads = split_heads(query_rows, head_count)
    key_heads = split_heads(key_rows, head_count)
    value_heads = split_heads(value_rows, head_count)
    grad_heads = split_heads(grad_mixed, head_count)
    score_scale = query_heads.shape[2] ** (-0.5)
    grad_probs = jnp.einsum(
        "qhd,khd->hqk", grad_heads, value_heads, preferred_element_type=jnp.float32
    )
    grad_values = jnp.einsum(
        "hqk,qhd->khd", probs_half, grad_heads, preferred_element_type=jnp.float32
    )
    inner = jnp.sum(attn_probs * grad_probs, axis=-1, keepdims=True)
    grad_scores = (attn_probs * (grad_probs - inner)).astype(jnp.bfloat16)
    grad_queries = (
        jnp.einsum("hqk,khd->qhd", grad_scores, key_heads, preferred_element_type=jnp.float32)
        * score_scale
    )
    grad_keys = (
        jnp.einsum("hqk,qhd->khd", grad_scores, query_heads, preferred_element_type=jnp.float32)
        * score_scale
    )
    pieces_list = [grad_queries, grad_keys, grad_values]
    return jnp.concatenate(
        [p.astype(jnp.bfloat16).reshape(row_count, -1) for p in pieces_list], axis=1
    )


def body(tokens, w_qkv, w_out, doc_blocks, cotangent):
    row_count = tokens.shape[0]
    head_width = w_out.shape[1]
    head_count = H
    all_devices = lax.axis_size("dp") * lax.axis_size("fsdp")
    allowed = row_mask(doc_blocks[0], row_count)
    columns = tokens
    qkv = jnp.dot(
        columns,
        lax.all_gather(w_qkv, "fsdp", axis=0, tiled=True),
        preferred_element_type=jnp.float32,
    ).astype(jnp.bfloat16)
    query_rows = qkv[:, :head_width]
    key_rows = qkv[:, head_width : 2 * head_width]
    value_rows = qkv[:, 2 * head_width :]
    mixed, attn_probs, probs_half = attend_forward(
        query_rows, key_rows, value_rows, allowed, head_count
    )
    output = lax.dot_general(
        mixed,
        lax.all_gather(w_out, "fsdp", axis=0, tiled=True),
        CONTRACT_COLS,
        preferred_element_type=jnp.float32,
    )
    columns = cotangent
    grad_mixed = jnp.dot(
        columns,
        lax.all_gather(w_out, "fsdp", axis=0, tiled=True),
        preferred_element_type=jnp.float32,
    ).astype(jnp.bfloat16)
    output = output.astype(jnp.bfloat16)
    grad_qkv = attend_backward(
        query_rows, key_rows, value_rows, attn_probs, probs_half, grad_mixed, head_count
    )
    grad_tokens = lax.dot_general(
        grad_qkv,
        lax.all_gather(w_qkv, "fsdp", axis=0, tiled=True),
        CONTRACT_COLS,
        preferred_element_type=jnp.float32,
    )
    grad_tokens = grad_tokens.astype(jnp.bfloat16)
    first_term = lax.dot_general(
        tokens, grad_qkv, CONTRACT_ROWS, preferred_element_type=jnp.float32
    )
    second_term = lax.dot_general(
        cotangent, mixed, CONTRACT_ROWS, preferred_element_type=jnp.float32
    )
    partial_grad = lax.psum_scatter(
        jnp.concatenate([first_term, second_term], axis=1), "fsdp", scatter_dimension=0, tiled=True
    )
    summed = lax.psum(partial_grad, "dp")
    norm_factor = 1.0 / math.sqrt(row_count * all_devices)
    grad_w_qkv = summed[:, : 3 * head_width] * norm_factor
    grad_w_out = summed[:, 3 * head_width :] * norm_factor
    return (output, grad_tokens, grad_w_qkv, grad_w_out)


def solution(mesh):
    placed = (
        P(("dp", "fsdp"), None),
        P("fsdp", None),
        P("fsdp", None),
        P(("dp", "fsdp"), None),
        P(("dp", "fsdp"), None),
    )
    return jax.shard_map(
        body,
        mesh=mesh,
        in_specs=placed,
        out_specs=(
            P(("dp", "fsdp"), None),
            P(("dp", "fsdp"), None),
            P("fsdp", None),
            P("fsdp", None),
        ),
        check_vma=False,
    )
```

profile of v0, /device:TPU:0, one launch (start us, length us, event | category | flops | bytes accessed | tf_op | source)
XLA Modules:
  0.0 596.9 jit_solution(12965069515736910643)
XLA Ops:
  8.7 1.4 fusion.30
  10.1 2.6 compare_select_fusion.1
  13.0 45.0 %all-gather.5.cloned.1.call-done = bf16[1024,1024]{1,0:T(8,128)(2,1)} async-done(((bf16[256,1024]{1,0:T(8,128)(2,1)}), bf16[1024,1024]{1,0:T(8,128)(2,1)}) %all-gather.5.cloned.1.call-update) | async-done | bytes 2097168 | tf_op jit(solution)/shard_map/all_gather | solution.py:95
  58.0 3.2 convolution_convert_fusion.1
  61.1 1.3 copy.29
  62.5 111.2 %all-gather.3.cloned.1.call-done = bf16[1024,3072]{1,0:T(8,128)(2,1)} async-done(((bf16[256,3072]{1,0:T(8,128)(2,1)}), bf16[1024,3072]{1,0:T(8,128)(2,1)}) %all-gather.3.cloned.1.call-update) | async-done | bytes 6291472 | tf_op jit(solution)/shard_map/all_gather | solution.py:84
  173.7 6.4 %convolution_convert_fusion = bf16[512,3072]{1,0:T(8,128)(2,1)S(1)} fusion(bf16[512,1024]{1,0:T(8,128)(2,1)S(1)} %copy-done, bf16[1024,3072]{1,0:T(8,128)(2,1)} %all-gather.3.cloned.1.call-done), kind=kOutput, calls=%fused_computation.8 | convolution fusion | flops 3222798336 | bytes 10485760 | tf_op jit(solution)/shard_map/dot_general | solution.py:82
  180.1 1.8 fusion.29
  182.5 1.5 copy.28
  184.0 5.4 fusion.31
  189.4 4.7 fusion.9
  194.2 1.7 copy-done.1
  196.1 1.5 fusion.12
  197.7 1.5 multiply_reduce_fusion
  199.2 2.7 multiply_convert_fusion
  201.9 1.5 multiply_convert_fusion.1
  206.3 3.5 convolution_bitcast_fusion
  209.8 7.2 %pad_maximum_fusion = f32[1024,4096]{0,1:T(8,128)} fusion(f32[1024,1024]{0,1:T(8,128)S(1)} %convolution_bitcast_fusion.1, f32[1024,3072]{0,1:T(8,128)S(1)} %convolution_bitcast_fusion), kind=kLoop, calls=%fused_computation.1 | loop fusion | flops 4194304 | bytes 33554432 | tf_op jit(solution)/shard_map/concatenate | solution.py:123
  217.2 278.7 %reduce-scatter.2.cloned.1.call-done = f32[256,4096]{0,1:T(8,128)} async-done(((f32[1024,4096]{0,1:T(8,128)}), f32[256,4096]{0,1:T(8,128)}) %reduce-scatter.2.cloned.1.call-update) | async-done | bytes 4194320 | tf_op jit(solution)/shard_map/reduce_scatter | solution.py:122
  495.9 4.0 convolution_convert_fusion.2
  499.9 7.2 %convolution_convert_fusion.3 = bf16[512,1024]{1,0:T(8,128)(2,1)} fusion(bf16[1024,3072]{1,0:T(8,128)(2,1)} %all-gather.3.cloned.1.call-done, bf16[512,1024]{0,1:T(8,128)(2,1)S(1)} %bitcast.77, bf16[512,1024]{0,1:T(8,128)(2,1)S(1)} %bitcast.70, bf16[512,1024]{0,1:T(8,128)(2,1)S(1)} %bitcast.72), kind=kOutput, calls=%fused_computation.26 | convolution fusion | flops 3231186944 | bytes 10485760 | tf_op jit(solution)/shard_map/dot_general | solution.py:109
  507.1 73.3 %all-reduce.2.cloned.1.call-done = f32[256,4096]{0,1:T(8,128)} async-done(((f32[256,4096]{0,1:T(8,128)}), f32[256,4096]{0,1:T(8,128)}) %all-reduce.2.cloned.1.call-update) | async-done | bytes 4194320 | tf_op jit(solution)/shard_map/psum | solution.py:125
  580.4 3.8 slice_multiply_fusion
  584.2 3.5 copy.21
  (38 shorter events, 8.1 us)
Async XLA Ops:
  7.2 166.5 %copy-start = (bf16[512,1024]{1,0:T(8,128)(2,1)S(1)}, bf16[512,1024]{1,0:T(8,128)(2,1)}, u32[]{:S(2)}) copy-start(bf16[512,1024]{1,0:T(8,128)(2,1)} %param.7) | copy-start | bytes 3145732
  7.2 50.8 %all-gather.5.cloned.1.call-start = ((), (), s32[]{:S(2)}) async-start(), calls=%async_computation.2 | async-start | bytes 2621440 | tf_op jit(solution)/shard_map/all_gather | solution.py:95
  7.9 165.8 %all-gather.3.cloned.1.call-start = ((), (), s32[]{:S(2)}) async-start(), calls=%async_computation.1 | async-start | bytes 7864320 | tf_op jit(solution)/shard_map/all_gather | solution.py:84
  8.7 487.2 %reduce-scatter.2.cloned.1.call-start = ((), (), s32[]{:S(2)}) async-start(), calls=%async_computation.3 | async-start | bytes 20971520 | tf_op jit(solution)/shard_map/reduce_scatter | solution.py:122
  189.4 6.5 %copy-start.1 = (f32[8,512,512]{1,2,0:T(8,128)S(1)}, f32[8,512,512]{1,2,0:T(8,128)}, u32[]{:S(2)}) copy-start(f32[8,512,512]{1,2,0:T(8,128)} %get-tuple-element.28) | copy-start | bytes 25165828
  189.4 6.7 %copy-start.2 = (bf16[512,1024]{0,1:T(8,128)(2,1)S(1)}, bf16[512,1024]{0,1:T(8,128)(2,1)}, u32[]{:S(2)}) copy-start(bf16[512,1024]{0,1:T(8,128)(2,1)} %copy.29) | copy-start | bytes 3145732
  194.1 10.0 %copy-start.9 = (bf16[8,128,512]{2,1,0:T(8,128)(2,1)}, bf16[8,128,512]{2,1,0:T(8,128)(2,1)S(1)}, u32[]{:S(2)}) copy-start(bf16[8,128,512]{2,1,0:T(8,128)(2,1)S(1)} %fusion.9) | copy-start | bytes 3145732
  196.1 1.5 copy-start.5
  197.6 8.6 %copy-start.7 = (bf16[8,128,512]{2,1,0:T(8,128)(2,1)}, bf16[8,128,512]{2,1,0:T(8,128)(2,1)S(1)}, u32[]{:S(2)}) copy-start(bf16[8,128,512]{2,1,0:T(8,128)(2,1)S(1)} %fusion.12) | copy-start | bytes 3145732
  203.4 2.9 copy-start.3
  203.4 1.6 copy-start.6
  217.1 278.8 %copy-start.10 = (bf16[8,128,512]{2,1,0:T(8,128)(2,1)S(1)}, bf16[8,128,512]{2,1,0:T(8,128)(2,1)}, u32[]{:S(2)}) copy-start(bf16[8,128,512]{2,1,0:T(8,128)(2,1)} %copy-done.9) | copy-start | bytes 3145732
  217.1 363.3 %all-reduce.2.cloned.1.call-start = ((), (), s32[]{:S(2)}) async-start(), calls=%async_computation.4 | async-start | bytes 8388608 | tf_op jit(solution)/shard_map/psum | solution.py:125
  495.9 4.0 copy-start.4
  495.9 4.0 copy-start.8
Sparse Core Ops, SparseCore 0:
  9.6 48.3 all-gather.4
  59.5 114.1 all-gather.2
  217.2 278.5 reduce-scatter.1
  499.0 81.4 all-reduce.1
where the time goes:
time: 597 us
  waiting for transfers between devices  510 us (85%)
  matrix products  41 us (7%)
  other arithmetic  17.8 us (3%)
  local copies, waits for them, and re-layouts  14.3 us (2%)
  between operations  14 us (2%)
    reduce_scatter x1, waiting for transfers between devices, body(): lax.psum_scatter(jnp.concatenate([first_term, second_term], axis=1), 'fsd...  279 us
    all_gather x1, waiting for transfers between devices, body(): lax.all_gather(w_qkv, 'fsdp', axis=0, tiled=True)  111 us
    psum x1, waiting for transfers between devices, body(): summed = lax.psum(partial_grad, 'dp')  73.3 us
    all_gather x1, waiting for transfers between devices, body(): lax.all_gather(w_out, 'fsdp', axis=0, tiled=True)  45 us
  transfers between devices with their start and end apart: 4, of which 4 were waited for; matrix products, arithmetic and copies ran while one was open for 3% of the time, Pallas kernels for 0%

commit v1 on v0

--- a/solution.py
+++ b/solution.py
@@ -73,6 +73,15 @@
 
 
 def body(tokens, w_qkv, w_out, doc_blocks, cotangent):
+
+    def close_lines(z_in):
+        extent = lax.axis_size("dp")
+        next_value = z_in
+        for k in [dev for dev in (1, 2, 4, 8, 16) if dev < extent]:
+            val = lax.ppermute(next_value, "dp", [(no, no ^ k) for no in range(extent)])
+            next_value = next_value + val
+        return next_value
+
     row_count = tokens.shape[0]
     head_width = w_out.shape[1]
     head_count = H
@@ -122,7 +131,7 @@
     partial_grad = lax.psum_scatter(
         jnp.concatenate([first_term, second_term], axis=1), "fsdp", scatter_dimension=0, tiled=True
     )
-    summed = lax.psum(partial_grad, "dp")
+    summed = close_lines(partial_grad)
     norm_factor = 1.0 / math.sqrt(row_count * all_devices)
     grad_w_qkv = summed[:, : 3 * head_width] * norm_factor
     grad_w_out = summed[:, 3 * head_width :] * norm_factor

time: 597 us -> 706 us (1.18)
  waiting for transfers between devices: 510 us -> 619 us
    ppermute x0 -> x3, waiting for transfers between devices: none -> 182 us  [close_lines(): val = lax.ppermute(next_value, 'dp', [(no, no ^ k) for no in range(extent)])]
    psum x1 -> x0, waiting for transfers between devices: 73.3 us -> none  [body(): summed = lax.psum(partial_grad, 'dp')]
  transfers between devices with their start and end apart: 4 -> 6, of which waited for: 4 -> 6; matrix products, arithmetic and copies ran while one was open for 3% -> 2% of each run, Pallas kernels for 0% -> 0%
where the time goes in v1:
time: 706 us; the launch traced here: 705 us
  waiting for transfers between devices  619 us (88%)
  matrix products  36.6 us (5%)
  other arithmetic  18.6 us (3%)
  local copies, waits for them, and re-layouts  14.4 us (2%)
  between operations  14 us (2%)
    reduce_scatter x1, waiting for transfers between devices, body(): lax.psum_scatter(jnp.concatenate([first_term, second_term], axis=1), 'fsd...  279 us
    ppermute x3, waiting for transfers between devices, close_lines(): val = lax.ppermute(next_value, 'dp', [(no, no ^ k) for no in range(extent)])  182 us
    all_gather x1, waiting for transfers between devices, body(): lax.all_gather(w_qkv, 'fsdp', axis=0, tiled=True)  111 us
    all_gather x1, waiting for transfers between devices, body(): lax.all_gather(w_out, 'fsdp', axis=0, tiled=True)  45 us
  transfers between devices with their start and end apart: 6, of which 6 were waited for; matrix products, arithmetic and copies ran while one was open for 2% of the time, Pallas kernels for 0%

profile of v1, /device:TPU:0, one launch (start us, length us, event | category | flops | bytes accessed | tf_op | source)
XLA Modules:
  0.0 705.2 jit_solution(4440395424994972814)
XLA Ops:
  10.1 2.6 compare_select_fusion.1
  13.0 45.0 %all-gather.5.cloned.1.call-done = bf16[1024,1024]{1,0:T(8,128)(2,1)} async-done(((bf16[256,1024]{1,0:T(8,128)(2,1)}), bf16[1024,1024]{1,0:T(8,128)(2,1)}) %all-gather.5.cloned.1.call-update) | async-done | bytes 2097168 | tf_op jit(solution)/shard_map/all_gather | solution.py:104
  58.0 3.2 convolution_convert_fusion.1
  62.5 111.2 %all-gather.3.cloned.1.call-done = bf16[1024,3072]{1,0:T(8,128)(2,1)} async-done(((bf16[256,3072]{1,0:T(8,128)(2,1)}), bf16[1024,3072]{1,0:T(8,128)(2,1)}) %all-gather.3.cloned.1.call-update) | async-done | bytes 6291472 | tf_op jit(solution)/shard_map/all_gather | solution.py:93
  173.7 6.4 convolution_convert_fusion
  180.1 1.8 fusion.29
  184.0 5.4 fusion.31
  189.4 4.7 fusion.9
  194.2 1.7 copy-done.2
  196.1 1.5 fusion.12
  199.2 2.7 multiply_convert_fusion
  206.3 3.5 convolution_bitcast_fusion
  209.9 7.2 %pad_maximum_fusion = f32[1024,4096]{0,1:T(8,128)} fusion(f32[1024,1024]{0,1:T(8,128)S(1)} %convolution_bitcast_fusion.1, f32[1024,3072]{0,1:T(8,128)S(1)} %convolution_bitcast_fusion), kind=kLoop, calls=%fused_computation.1 | loop fusion | flops 4194304 | bytes 33554432 | tf_op jit(solution)/shard_map/concatenate | solution.py:132
  217.1 278.9 %reduce-scatter.2.cloned.1.call-done = f32[256,4096]{0,1:T(8,128)} async-done(((f32[1024,4096]{0,1:T(8,128)}), f32[256,4096]{0,1:T(8,128)}) %reduce-scatter.2.cloned.1.call-update) | async-done | bytes 4194320 | tf_op jit(solution)/shard_map/reduce_scatter | solution.py:131
  495.9 7.4 %collective-permute-done = f32[256,4096]{0,1:T(8,128)S(1)} collective-permute-done((f32[256,4096]{0,1:T(8,128)}, f32[256,4096]{0,1:T(8,128)S(1)}, u32[]{:S(2)}, u32[]{:S(2)}) %collective-permute-start) | collective-permute-done | bytes 4194336 | tf_op jit(solution)/shard_map/ppermute | solution.py:81
  503.3 2.9 add.78
  506.2 1.5 collective-permute-start.1
  507.8 91.1 %collective-permute-done.1 = f32[256,4096]{0,1:T(8,128)S(1)} collective-permute-done((f32[256,4096]{0,1:T(8,128)S(1)}, f32[256,4096]{0,1:T(8,128)S(1)}, u32[]{:S(2)}, u32[]{:S(2)}) %collective-permute-start.1) | collective-permute-done | bytes 4194336 | tf_op jit(solution)/shard_map/ppermute | solution.py:81
  599.5 1.5 collective-permute-start.2
  601.0 2.3 convolution_convert_fusion.2
  603.3 4.4 convolution_convert_fusion.3
  607.8 83.5 %collective-permute-done.2 = f32[256,4096]{0,1:T(8,128)S(1)} collective-permute-done((f32[256,4096]{0,1:T(8,128)S(1)}, f32[256,4096]{0,1:T(8,128)S(1)}, u32[]{:S(2)}, u32[]{:S(2)}) %collective-permute-start.2) | collective-permute-done | bytes 4194336 | tf_op jit(solution)/shard_map/ppermute | solution.py:81
  691.9 1.9 slice_multiply_fusion
  693.8 3.6 copy.21
  (53 shorter events, 15.1 us)
Async XLA Ops:
  7.2 166.5 %copy-start = (bf16[512,1024]{1,0:T(8,128)(2,1)S(1)}, bf16[512,1024]{1,0:T(8,128)(2,1)}, u32[]{:S(2)}) copy-start(bf16[512,1024]{1,0:T(8,128)(2,1)} %param.7) | copy-start | bytes 3145732
  7.2 50.8 %all-gather.5.cloned.1.call-start = ((), (), s32[]{:S(2)}) async-start(), calls=%async_computation.2 | async-start | bytes 2621440 | tf_op jit(solution)/shard_map/all_gather | solution.py:104
  7.9 165.8 %all-gather.3.cloned.1.call-start = ((), (), s32[]{:S(2)}) async-start(), calls=%async_computation.1 | async-start | bytes 7864320 | tf_op jit(solution)/shard_map/all_gather | solution.py:93
  8.7 487.3 %reduce-scatter.2.cloned.1.call-start = ((), (), s32[]{:S(2)}) async-start(), calls=%async_computation.3 | async-start | bytes 20971520 | tf_op jit(solution)/shard_map/reduce_scatter | solution.py:131
  189.4 6.5 copy-start.2
  189.4 6.7 copy-start.3
  194.2 10.0 %copy-start.11 = (bf16[8,128,512]{2,1,0:T(8,128)(2,1)}, bf16[8,128,512]{2,1,0:T(8,128)(2,1)S(1)}, u32[]{:S(2)}) copy-start(bf16[8,128,512]{2,1,0:T(8,128)(2,1)S(1)} %fusion.9) | copy-start | bytes 3145732
  196.1 1.5 copy-start.6
  197.7 8.6 %copy-start.9 = (bf16[8,128,512]{2,1,0:T(8,128)(2,1)}, bf16[8,128,512]{2,1,0:T(8,128)(2,1)S(1)}, u32[]{:S(2)}) copy-start(bf16[8,128,512]{2,1,0:T(8,128)(2,1)S(1)} %fusion.12) | copy-start | bytes 3145732
  203.4 2.9 copy-start.4
  203.4 1.6 copy-start.8
  495.9 7.4 %collective-permute-start = (f32[256,4096]{0,1:T(8,128)}, f32[256,4096]{0,1:T(8,128)S(1)}, u32[]{:S(2)}, u32[]{:S(2)}) collective-permute-start(f32[256,4096]{0,1:T(8,128)} %reduce-scatter.2.cloned.1.call-done), channel_id=1, source_target_pairs={{0,4},{4,0},{8,12},{12,8},{16,20},{20,16},{24,28},{28,24},{1,5},{5... | collective-permute-start | bytes 12582920 | tf_op jit(solution)/shard_map/ppermute | solution.py:81
  503.3 100.0 %slice-start = ((s8[6291456]{0:T(1024)(128)(4,1)}), s8[4194304]{0:T(1024)(128)(4,1)S(1)}, s32[]{:S(2)}) async-start(s8[6291456]{0:T(1024)(128)(4,1)} %bitcast.76), calls=%async_computation.4 | async-start | bytes 8388608
  506.2 94.8 %copy-start.7 = (bf16[1024,1024]{1,0:T(8,128)(2,1)S(1)}, bf16[1024,1024]{1,0:T(8,128)(2,1)}, u32[]{:S(2)}) copy-start(bf16[1024,1024]{1,0:T(8,128)(2,1)} %all-gather.5.cloned.1.call-done) | copy-start | bytes 6291460
  506.2 94.8 %copy-start.12 = (bf16[8,128,512]{2,1,0:T(8,128)(2,1)S(1)}, bf16[8,128,512]{2,1,0:T(8,128)(2,1)}, u32[]{:S(2)}) copy-start(bf16[8,128,512]{2,1,0:T(8,128)(2,1)} %copy-done.11) | copy-start | bytes 3145732
  506.2 97.1 %slice-start.1 = ((s8[6291456]{0:T(1024)(128)(4,1)}), s8[2097152]{0:T(1024)(128)(4,1)S(1)}, s32[]{:S(2)}) async-start(s8[6291456]{0:T(1024)(128)(4,1)} %bitcast.76), calls=%async_computation.5 | async-start | bytes 4194304
  506.2 92.7 %collective-permute-start.1 = (f32[256,4096]{0,1:T(8,128)S(1)}, f32[256,4096]{0,1:T(8,128)S(1)}, u32[]{:S(2)}, u32[]{:S(2)}) collective-permute-start(f32[256,4096]{0,1:T(8,128)S(1)} %add.78), channel_id=1, source_target_pairs={{0,8},{4,12},{8,0},{12,4},{16,24},{20,28},{24,16},{28,20},{1,9},{5... | collective-permute-start | bytes 12582920 | tf_op jit(solution)/shard_map/ppermute | solution.py:81
  599.5 3.9 copy-start.5
  599.5 3.8 copy-start.10
  599.5 91.8 %collective-permute-start.2 = (f32[256,4096]{0,1:T(8,128)S(1)}, f32[256,4096]{0,1:T(8,128)S(1)}, u32[]{:S(2)}, u32[]{:S(2)}) collective-permute-start(f32[256,4096]{0,1:T(8,128)S(1)} %add.79), channel_id=1, source_target_pairs={{0,16},{4,20},{8,24},{12,28},{16,0},{20,4},{24,8},{28,12},{1,17},{... | collective-permute-start | bytes 12582920 | tf_op jit(solution)/shard_map/ppermute | solution.py:81
  693.7 5.0 copy-start.1
Sparse Core Ops, SparseCore 0:
  9.6 48.3 all-gather.4
  59.5 114.1 all-gather.2
  217.2 278.6 reduce-scatter.1
